TPU v7x, 32 devices: a whole 2x2x4 slice. The times are simulated.
32 devices in a mesh: parts: 2 (over y), samp: 4 (over x, core), bond: 4 (over z).
Axes of the slice: x: 2, y: 2, z: 4, core: 2. Of those that a mesh axis runs over, the one named last changes fastest.
Arguments:
- env_start: bfloat16 [4096, 4096], P(('parts', 'samp'), 'bond'), parts along dimension 0, may hold values from -6 to 6
- stored_sites: bfloat16 [4, 4, 1024, 4, 4096], P('parts', 'samp', None, None, 'bond'), parts along dimension 0, may hold values from -1 to 1
- slab_order: int32 [4, 4], P('parts'), parts along dimension 0, may hold values from 0 to 3, each once within a row
- chosen: int32 [4096, 2], P(('parts', 'samp')), parts along dimension 0, may hold values from 0 to 3
Outputs:
- probabilities: float32 [4096, 2, 4], P(('parts', 'samp')), parts along dimension 0
- env_final: float32 [4096, 4096], P(('parts', 'samp'), 'bond'), parts along dimension 0
There are 2 independent parts, one for each index of `parts`. A program takes and returns all parts, laid end to end along the dimension named above; each array names one. Nothing has to cross between parts.
Inputs may be any that keep to these rules, and one draw needn't show every extreme that they name: Each row of slab_order names every index of samp once.
All inputs are finite; a program needn't handle non-finite values.
Results may differ from a plain program's by a relative error of at most 0.005.
Values may be sent and summed in bfloat16 or wider, within the bound.
A program may use at most 192 MiB of HBM per device.

v0:
```python
import functools

import jax
import jax.numpy as jnp
from jax import lax
from jax.experimental import pallas as pl
from jax.experimental.pallas import tpu as pltpu
from jax.sharding import PartitionSpec as P


STEPS = 2
CHUNKS = 2
PIECES = 2
epsilon = 1e-06


def tile_of(width):
    return min(width, 256)


def dots(env_ref, weight_refs, outcome):
    total = None
    for part, weight_ref in enumerate(weight_refs):
        term = jnp.dot(env_ref[part], weight_ref[outcome], preferred_element_type=jnp.float32)
        total = term if total is None else total + term
    return total


def product_kernel(count, env_ref, *refs):
    weight_refs, out_ref = refs[:count], refs[count]
    for outcome in range(out_ref.shape[0]):
        out_ref[outcome] = dots(env_ref, weight_refs, outcome).astype(out_ref.dtype)


def product(env, weights, piece, pieces, dtype):
    outcomes, rows, width = weights[0].shape
    count = outcomes // pieces
    samples, tile = env.shape[1], tile_of(width)
    flops = 2 * samples * sum(w.size for w in weights) // pieces
    moved = 2 * sum(w.size for w in weights) // pieces
    return pl.pallas_call(
        functools.partial(product_kernel, len(weights)),
        grid=(width // tile,),
        in_specs=[pl.BlockSpec(env.shape, lambda t: (0, 0, 0))]
        + [pl.BlockSpec((count, rows, tile), lambda t: (piece, 0, t)) for _ in weights],
        out_specs=pl.BlockSpec((count, samples, tile), lambda t: (0, 0, t)),
        out_shape=jax.ShapeDtypeStruct((count, samples, width), dtype),
        cost_estimate=pl.CostEstimate(flops=flops, bytes_accessed=moved, transcendentals=0),
    )(env, *weights)


def finish_kernel(pieces, site, own_ref, chosen_ref, before_ref, *refs):
    other_refs, (totals_ref, selected_ref) = refs[:-2], refs[-2:]
    outcomes = own_ref.shape[0]
    each = outcomes // pieces

    @pl.when(pl.program_id(0) == 0)
    def _():
        totals_ref[...] = before_ref[...]

    lane = lax.broadcasted_iota(jnp.int32, totals_ref.shape, 1)
    selected = None
    added = jnp.zeros(totals_ref.shape, jnp.float32)
    for outcome in range(outcomes):
        total = own_ref[outcome]
        for other_ref in other_refs[outcome // each :: pieces]:
            total = total + other_ref[outcome % each].astype(jnp.float32)
        norm = jnp.sum(total * total, axis=1, keepdims=True)
        added = jnp.where(lane == site * outcomes + outcome, norm, added)
        hit = chosen_ref[...] == outcome
        selected = jnp.where(hit, total, 0.0 if selected is None else selected)
    totals_ref[...] += added
    selected_ref[...] = selected.astype(selected_ref.dtype)


def finish(own, others, chosen, before, site, dtype):
    outcomes, samples, width = own.shape
    tile = tile_of(width)
    pieces = outcomes // others[0].shape[0] if others else 1
    return pl.pallas_call(
        functools.partial(finish_kernel, pieces, site),
        grid=(width // tile,),
        in_specs=[
            pl.BlockSpec((outcomes, samples, tile), lambda t: (0, 0, t)),
            pl.BlockSpec((samples, 1), lambda t: (0, 0)),
            pl.BlockSpec((samples, 128), lambda t: (0, 0)),
        ]
        + [pl.BlockSpec((outcomes // pieces, samples, tile), lambda t: (0, 0, t)) for _ in others],
        out_specs=(
            pl.BlockSpec((samples, 128), lambda t: (0, 0)),
            pl.BlockSpec((samples, tile), lambda t: (0, t)),
        ),
        out_shape=(
            jax.ShapeDtypeStruct((samples, 128), jnp.float32),
            jax.ShapeDtypeStruct((samples, width), dtype),
        ),
        cost_estimate=pl.CostEstimate(
            flops=4 * own.size, bytes_accessed=8 * own.size, transcendentals=0
        ),
    )(own, chosen, before, *others)


def relayout_kernel(stored_ref, _, out_ref):
    for outcome in range(out_ref.shape[0]):
        out_ref[outcome] = stored_ref[0, 0, :, outcome, :]


def relayout(stored_sites, site, after):
    rows, outcomes, width = stored_sites.shape[2:]
    tile = min(rows, 128)
    return pl.pallas_call(
        relayout_kernel,
        grid=(rows // tile,),
        in_specs=[
            pl.BlockSpec((1, 1, tile, outcomes, width), lambda t: (site, 0, t, 0, 0)),
            pl.BlockSpec(memory_space=pl.ANY),
        ],
        out_specs=pl.BlockSpec((outcomes, tile, width), lambda t: (0, t, 0)),
        out_shape=jax.ShapeDtypeStruct((outcomes, rows, width), stored_sites.dtype),
        cost_estimate=pl.CostEstimate(
            flops=0, bytes_accessed=4 * rows * outcomes * width, transcendentals=0
        ),
    )(stored_sites, after)


def pick_kernel(inner, index_ref, *refs):
    pieces, outs = refs[: len(refs) - inner[1]], refs[len(refs) - inner[1] :]
    for target, out_ref in enumerate(outs):
        for part in range(inner[0]):
            for source, piece_ref in enumerate(pieces):

                @pl.when(index_ref[target * inner[0] + part] == source)
                def _():
                    out_ref[part] = piece_ref[...]


def pick_blocks(index, pieces, outer, inner):
    samples, width = pieces[0].shape
    spec = pl.BlockSpec((samples, width), lambda t, index: (0, 0))
    return pl.pallas_call(
        functools.partial(pick_kernel, (inner, outer)),
        grid_spec=pltpu.PrefetchScalarGridSpec(
            num_scalar_prefetch=1,
            grid=(1,),
            in_specs=[spec] * len(pieces),
            out_specs=[pl.BlockSpec((inner, samples, width), lambda t, index: (0, 0, 0))] * outer,
        ),
        out_shape=[jax.ShapeDtypeStruct((inner, samples, width), pieces[0].dtype)] * outer,
        cost_estimate=pl.CostEstimate(
            flops=0, bytes_accessed=2 * samples * width * (len(pieces) + outer * inner), transcendentals=0
        ),
    )(index, *pieces)


def compute(env_start, stored_sites, slab_order, chosen):
    groups = slab_order.shape[1]
    inner = 2 if groups % 2 == 0 else 1
    outer = groups // inner
    bonds = lax.axis_size("bond")
    mine, place = lax.axis_index("samp"), lax.axis_index("bond")
    core, chip = mine % inner, mine // inner
    rows, outcomes, width = stored_sites.shape[2:]
    bond_width = width * bonds
    samples = env_start.shape[0]
    chunks = CHUNKS if samples % (CHUNKS * 16) == 0 else 1
    size = samples // chunks

    def across(value, step):
        return lax.ppermute(
            value, "samp", [(i, ((i // inner + step) % outer) * inner + i % inner) for i in range(groups)]
        )

    def inside(value, step):
        return lax.ppermute(
            value, "samp", [((i // inner) * inner + (i + step) % inner, i) for i in range(groups)]
        )

    def along(value, step):
        return lax.ppermute(value, "bond", [(i, (i + step) % bonds) for i in range(bonds)])

    def load(site, after):
        own = relayout(stored_sites, site, after)
        return [own] + [inside(own, step) for step in range(1, inner)]

    wanted = [
        jnp.stack(
            [
                slab_order[site, ((chip + step) % outer) * inner + (core + part) % inner]
                for step in range(outer)
                for part in range(inner)
            ]
        )
        for site in range(STEPS)
    ]

    def gather(value, site):
        if bonds == groups:
            pieces = [value] + [along(value, step) for step in range(1, bonds)]
            index = (place - wanted[site] + bonds) % bonds
            return lambda: pick_blocks(index, pieces, outer, inner)
        whole = lax.all_gather(value, "bond", axis=1, tiled=True)
        blocks = [
            lax.dynamic_slice_in_dim(whole, wanted[site][i] * rows, rows, axis=1)
            for i in range(groups)
        ]
        return lambda: [
            jnp.stack(blocks[step * inner : (step + 1) * inner]) for step in range(outer)
        ]

    def bond_sum(value):
        if bonds <= 4:
            return sum([along(value, step) for step in range(1, bonds)], value)
        return lax.psum(value, "bond")

    raws = [env_start[c * size : (c + 1) * size] for c in range(chunks)]
    picks = [chosen[c * size : (c + 1) * size] for c in range(chunks)]
    norms = [jnp.zeros((size, 128), jnp.float32)] * chunks

    def fetch(value, site):
        pick = gather(value, site)
        own, *foreign = pick()
        return own, [(i + 1, across(block, i + 1)) for i, block in enumerate(foreign)]

    owns, sents = [], []
    for c in range(chunks):
        own, sent = fetch(raws[c], 0)
        owns.append(own)
        sents.append(sent)
    weights = load(0, norms[0])
    for site in range(STEPS):
        last = site + 1 == STEPS
        answers = []
        for c in range(chunks):
            parts, anchor = [], norms[0]
            for step, foreign in sents[c]:
                for piece in range(PIECES):
                    anchor = product(foreign, weights, piece, PIECES, jnp.bfloat16)
                    parts.append(across(anchor, -step))
            answers.append(parts)
            if c == 0 and not last:
                later = load(site + 1, anchor)
        new_owns, new_sents = [], []
        for c in range(chunks):
            own = product(owns[c], weights, 0, 1, jnp.float32)
            norms[c], raws[c] = finish(
                own,
                answers[c],
                picks[c][:, site : site + 1],
                norms[c],
                site,
                jnp.float32 if last else jnp.bfloat16,
            )
            if not last:
                own, sent = fetch(raws[c], site + 1)
                new_owns.append(own)
                new_sents.append(sent)
        if not last:
            owns, sents, weights = new_owns, new_sents, later
    sums = [bond_sum(norm) for norm in norms]
    totals = [[s[:, site * outcomes : (site + 1) * outcomes] for s in sums] for site in range(STEPS)]
    probabilities, finals = [], []
    labels = jnp.arange(outcomes, dtype=jnp.int32)
    for c in range(chunks):
        factor = jnp.ones((size,), jnp.float32)
        rows_out = []
        for site in range(STEPS):
            scaled = totals[site][c] * (factor * factor)[:, None]
            rows_out.append(scaled / jnp.sum(scaled, axis=1, keepdims=True))
            hit = picks[c][:, site][:, None] == labels[None, :]
            factor = factor * lax.rsqrt(jnp.sum(jnp.where(hit, scaled, 0.0), axis=1) / bond_width + epsilon)
        probabilities.append(jnp.stack(rows_out, axis=1))
        finals.append(raws[c] * factor[:, None])
    return jnp.concatenate(probabilities), jnp.concatenate(finals)


MESH = pl.DeviceIdType.MESH
PARTS_OF_SITE = 4
SHARE = 4
LEAD = 3


def sampling_kernel(
    bonds, groups, mask_ref, env_ref, stored_ref, chosen_ref, selected_ref, totals_ref,
    weights, blocks, foreign, picked, partial, answer, own, left, stage, norms, gathered,
    env_sem, stage_sem, weight_send, weight_recv, gather_send, gather_recv, cross_send, cross_recv,
    spread_send, spread_recv, answer_send, answer_recv, norm_send, norm_recv,
):
    mine, place = lax.axis_index("samp"), lax.axis_index("bond")
    core = lax.rem(mine, 2)
    sibling, opposite = mine + 1 - 2 * core, lax.rem(mine + groups // 2, groups)
    peers = (None, place + 1 - 2 * lax.rem(place, 2), lax.rem(place + 2, bonds), bonds - 1 - place)
    middle = lax.div(place + 1, 2) == 1
    outer = lax.div(place + 1, 2) != 1
    outcomes = weights.shape[2]
    width = weights.shape[4]
    chunks = PARTS_OF_SITE
    rows = left.shape[1] // 2
    share = rows // SHARE
    units = STEPS * chunks
    slab = weights.shape[3]
    tall = stage.shape[1]
    tiles = slab // tall
    strip = min(width, 256)
    band = min(rows, 16)

    def copy_to(src, dst, send, recv, where):
        return pltpu.make_async_remote_copy(
            src_ref=src, dst_ref=dst, send_sem=send, recv_sem=recv, device_id=where, device_id_type=MESH
        )

    def split(unit):
        return lax.div(unit, chunks), lax.rem(unit, chunks)

    def spot(chunk):
        return pl.ds(pl.multiple_of(chunk * rows, rows), rows)

    def hop(unit, d):
        site, chunk = split(unit)
        ref = blocks.at[site, place, spot(chunk)]
        return copy_to(ref, ref, gather_send.at[unit, d - 1], gather_recv.at[unit, d - 1], {"bond": peers[d]})

    def relay(unit):
        site, chunk = split(unit)
        ref = blocks.at[site, peers[3], spot(chunk)]
        return copy_to(ref, ref, gather_send.at[unit, 1], gather_recv.at[unit, 1], {"bond": peers[1]})

    def cross_whole(unit):
        return copy_to(
            picked.at[lax.rem(unit, 2)],
            foreign.at[lax.rem(unit, chunks)],
            cross_send.at[unit],
            cross_recv.at[unit],
            {"samp": opposite},
        )

    def band_of(position):
        return pl.ds(pl.multiple_of(position * share, share), share)

    def cross_part(unit):
        return copy_to(
            picked.at[lax.rem(unit, 2), :, pl.ds(0, share)],
            foreign.at[lax.rem(unit, chunks), :, band_of(lax.rem(place, SHARE))],
            cross_send.at[unit],
            cross_recv.at[unit],
            {"samp": opposite},
        )

    def spread(unit, d):
        ref = foreign.at[lax.rem(unit, chunks), :, band_of(lax.rem(place, SHARE))]
        return copy_to(ref, ref, spread_send.at[unit, d - 1], spread_recv.at[unit, d - 1], {"bond": peers[d]})

    def reply(unit, outcome):
        return copy_to(
            partial.at[lax.rem(unit, 2), outcome],
            answer.at[lax.rem(unit, chunks), outcome],
            answer_send.at[unit, outcome],
            answer_recv.at[unit, outcome],
            {"samp": opposite},
        )

    def load(index):
        return pltpu.make_async_copy(
            stored_ref.at[lax.div(index, tiles), 0, pl.ds(lax.rem(index, tiles) * tall, tall)],
            stage.at[lax.rem(index, 2)],
            stage_sem.at[lax.rem(index, 2)],
        )

    def trade(index):
        site, at = lax.div(index, tiles), pl.ds(pl.multiple_of(lax.rem(index, tiles) * tall, tall), tall)
        return copy_to(
            weights.at[site, 0, :, at],
            weights.at[site, 1, :, at],
            weight_send.at[site],
            weight_recv.at[site],
            {"samp": sibling},
        )

    def trade_all(site):
        return copy_to(
            weights.at[site, 0], weights.at[site, 1], weight_send.at[site], weight_recv.at[site], {"samp": sibling}
        )

    def pick(site, which, at):
        total = None
        for block in range(bonds):
            term = blocks[site, block, at, :].astype(jnp.float32) * mask_ref[(site * 4 + which) * bonds + block]
            total = term if total is None else total + term
        return total.astype(left.dtype)

    def send_blocks(unit):
        hop(unit, 1).start()
        hop(unit, 3).start()

        @pl.when(outer)
        def _():
            hop(unit, 2).start()

    def forward_block(unit):
        @pl.when(middle)
        def _():
            hop(unit, 3).wait_recv()
            relay(unit).start()

    def send_foreign(unit):
        site, chunk = split(unit)
        hop(unit, 1).wait_recv()
        hop(unit, 2).wait_recv()

        @pl.when(outer)
        def _():
            hop(unit, 3).wait_recv()

        slot = lax.rem(unit, 2)

        @pl.when(unit == 2)
        def _():
            cross_whole(unit - 2).wait_send()

        @pl.when(unit > 2)
        def _():
            cross_part(unit - 2).wait_send()

        @pl.when(unit == 0)
        def _():
            for part in range(2):

                @pl.loop(0, rows // band)
                def _(step):
                    at = pl.multiple_of(step * band, band)
                    picked[slot, part, pl.ds(at, band), :] = pick(site, 2 + part, pl.ds(chunk * rows + at, band))

            cross_whole(unit).start()

        @pl.when(unit > 0)
        def _():
            at = pl.multiple_of(chunk * rows + lax.rem(place, SHARE) * share, share)
            for part in range(2):
                picked[slot, part, pl.ds(0, share), :] = pick(site, 2 + part, pl.ds(at, share))
            cross_part(unit).start()

    def spread_foreign(unit):
        @pl.when(unit > 0)
        def _():
            cross_part(unit).wait_recv()
            for d in range(1, SHARE):
                spread(unit, d).start()

    def multiply(unit):
        site, chunk = split(unit)
        slot = lax.rem(unit, 2)

        for part in range(2):

            @pl.loop(0, rows // band)
            def _(step):
                at = pl.multiple_of(step * band, band)
                left[part, pl.ds(rows + at, band), :] = pick(site, part, pl.ds(chunk * rows + at, band))

        @pl.when(unit == 0)
        def _():
            cross_whole(unit).wait_recv()

        @pl.when(unit > 0)
        def _():
            for d in range(1, SHARE):
                spread(unit, d).wait_recv()
            for d in range(1, SHARE):
                spread(unit, d).wait_send()

        for part in range(2):
            left[part, pl.ds(0, rows), :] = foreign[chunk, part]

        @pl.when(chunk == 0)
        def _():
            trade_all(site).wait_recv()

        @pl.loop(0, outcomes)
        def _(outcome):
            @pl.when((outcome == outcomes // 2) & (unit + 1 < units))
            def _():
                spread_foreign(unit + 1)

            @pl.when(unit >= 2)
            def _():
                reply(unit - 2, outcome).wait_send()

            @pl.loop(0, width // strip)
            def _(step):
                at = pl.ds(pl.multiple_of(step * strip, strip), strip)
                total = jnp.dot(left[0], weights[site, 0, outcome, :, at], preferred_element_type=jnp.float32)
                total = total + jnp.dot(left[1], weights[site, 1, outcome, :, at], preferred_element_type=jnp.float32)
                partial[slot, outcome, :, at] = total[:rows].astype(partial.dtype)
                own[slot, outcome, :, at] = total[rows:]

            reply(unit, outcome).start()

    def finish(unit):
        site, chunk = split(unit)
        slot = lax.rem(unit, 2)

        @pl.loop(0, outcomes)
        def _(outcome):
            reply(unit, outcome).wait_recv()

            @pl.loop(0, rows // band)
            def _(step):
                at = pl.ds(pl.multiple_of(step * band, band), band)
                to = pl.ds(pl.multiple_of(chunk * rows + step * band, band), band)
                total = own[slot, outcome, at, :] + answer[chunk, outcome, at, :].astype(jnp.float32)
                norm = jnp.sum(total * total, axis=1, keepdims=True)
                lane = lax.broadcasted_iota(jnp.int32, (band, norms.shape[1]), 1)
                norms[to, :] = jnp.where(lane == site * outcomes + outcome, norm, norms[to, :])
                selected_ref[to, :] = jnp.where(chosen_ref[site, to, :] == outcome, total, selected_ref[to, :])

        @pl.when(site + 1 < STEPS)
        def _():
            @pl.loop(0, rows // band)
            def _(step):
                to = pl.ds(pl.multiple_of(chunk * rows + step * band, band), band)
                blocks[site + 1, place, to, :] = selected_ref[to, :].astype(blocks.dtype)

    def shuffle(index):
        load(index).wait()

        @pl.when(index + 1 < STEPS * tiles)
        def _():
            load(index + 1).start()

        site, at = lax.div(index, tiles), pl.ds(pl.multiple_of(lax.rem(index, tiles) * tall, tall), tall)
        slot = lax.rem(index, 2)
        for outcome in range(outcomes):
            weights[site, 0, outcome, at, :] = stage[slot, :, outcome, :]
        trade(index).start()

    first = pltpu.make_async_copy(env_ref, blocks.at[0, place], env_sem)
    first.start()
    load(0).start()
    barrier = pltpu.get_barrier_semaphore()
    friends = [{"bond": peers[d]} for d in range(1, bonds)] + [{"samp": sibling}, {"samp": opposite}]
    for friend in friends:
        pl.semaphore_signal(barrier, inc=1, device_id=friend, device_id_type=MESH)
    norms[...] = jnp.zeros_like(norms)
    selected_ref[...] = jnp.zeros_like(selected_ref)
    first.wait()
    pl.semaphore_wait(barrier, len(friends))

    each = -(-STEPS * tiles // (2 * LEAD))

    @pl.loop(0, units + LEAD + 1)
    def _(step):
        now = step - LEAD

        @pl.when((now + 2 >= 0) & (now + 2 < units))
        def _():
            forward_block(now + 2)

        @pl.when((now + 1 >= 0) & (now + 1 < units))
        def _():
            send_foreign(now + 1)

        @pl.when((now >= 0) & (now < units))
        def _():
            multiply(now)

        @pl.when(now >= 1)
        def _():
            finish(now - 1)

        @pl.when(now + 3 < units)
        def _():
            send_blocks(now + 3)

        @pl.loop(0, each)
        def _(turn):
            index = step * each + turn

            @pl.when(index < STEPS * tiles)
            def _():
                shuffle(index)

    for chunk in range(chunks):
        at = pl.ds(chunk * rows, rows)
        gathered[place, :, at] = jnp.transpose(norms[at, :])[: STEPS * outcomes]
    sums = []
    for d in range(1, bonds):
        ref = gathered.at[place]
        sums.append(copy_to(ref, ref, norm_send.at[d - 1], norm_recv.at[d - 1], {"bond": peers[d]}))
    for one in sums:
        one.start()
    for site in range(STEPS):
        trade_all(site).wait_send()

    @pl.loop(0, units)
    def _(unit):
        for d in range(1, bonds):
            hop(unit, d).wait_send()

    for unit in range(units - 2, units):
        cross_part(unit).wait_send()
        for outcome in range(outcomes):
            reply(unit, outcome).wait_send()
    for one in sums:
        one.wait()
    totals_ref[...] = gathered[0] + gathered[1] + gathered[2] + gathered[3]


def sample_sites(env_start, stored_sites, slab_order, chosen):
    groups, bonds = slab_order.shape[1], lax.axis_size("bond")
    mine = lax.axis_index("samp")
    slab, outcomes, width = stored_sites.shape[2:]
    samples = env_start.shape[0]
    rows = samples // PARTS_OF_SITE
    units = STEPS * PARTS_OF_SITE
    tall = min(slab, 128)
    sibling, opposite = mine + 1 - 2 * (mine % 2), (mine + groups // 2) % groups
    opposite_sibling = opposite + 1 - 2 * (opposite % 2)
    wanted = slab_order[:, jnp.stack([mine, sibling, opposite, opposite_sibling])]
    mask = (wanted[:, :, None] == jnp.arange(bonds, dtype=jnp.int32)).astype(jnp.float32).reshape(-1)
    kind = env_start.dtype
    dma = pltpu.SemaphoreType.DMA
    selected, totals = pl.pallas_call(
        functools.partial(sampling_kernel, bonds, groups),
        in_specs=[
            pl.BlockSpec(memory_space=pltpu.SMEM),
            pl.BlockSpec(memory_space=pl.ANY),
            pl.BlockSpec(memory_space=pl.ANY),
            pl.BlockSpec(memory_space=pltpu.VMEM),
        ],
        out_specs=(pl.BlockSpec(memory_space=pltpu.VMEM), pl.BlockSpec(memory_space=pltpu.VMEM)),
        out_shape=(
            jax.ShapeDtypeStruct((samples, width), jnp.float32),
            jax.ShapeDtypeStruct((STEPS * outcomes, samples), jnp.float32),
        ),
        scratch_shapes=[
            pltpu.VMEM((STEPS, 2, outcomes, slab, width), kind),
            pltpu.VMEM((STEPS, bonds, samples, width), kind),
            pltpu.VMEM((PARTS_OF_SITE, 2, rows, width), kind),
            pltpu.VMEM((2, 2, rows, width), kind),
            pltpu.VMEM((2, outcomes, rows, width), kind),
            pltpu.VMEM((PARTS_OF_SITE, outcomes, rows, width), kind),
            pltpu.VMEM((2, outcomes, rows, width), jnp.float32),
            pltpu.VMEM((2, 2 * rows, width), kind),
            pltpu.VMEM((2, tall, outcomes, width), kind),
            pltpu.VMEM((samples, 128), jnp.float32),
            pltpu.VMEM((bonds, STEPS * outcomes, samples), jnp.float32),
            dma,
            dma((2,)),
            dma((STEPS,)),
            dma((STEPS,)),
            dma((units, bonds - 1)),
            dma((units, bonds - 1)),
            dma((units,)),
            dma((units,)),
            dma((units, bonds - 1)),
            dma((units, bonds - 1)),
            dma((units, outcomes)),
            dma((units, outcomes)),
            dma((bonds - 1,)),
            dma((bonds - 1,)),
        ],
        compiler_params=pltpu.CompilerParams(
            collective_id=0, has_side_effects=True, vmem_limit_bytes=67_000_000
        ),
    )(mask, env_start, stored_sites, jnp.transpose(chosen)[:, :, None])
    totals = jnp.transpose(totals).reshape(samples, STEPS, outcomes)
    factor = jnp.ones((samples,), jnp.float32)
    labels = jnp.arange(outcomes, dtype=jnp.int32)
    probabilities = []
    for site in range(STEPS):
        scaled = totals[:, site] * (factor * factor)[:, None]
        probabilities.append(scaled / jnp.sum(scaled, axis=1, keepdims=True))
        hit = chosen[:, site][:, None] == labels[None, :]
        factor = factor * lax.rsqrt(jnp.sum(jnp.where(hit, scaled, 0.0), axis=1) / (width * bonds) + epsilon)
    return jnp.stack(probabilities, axis=1), selected * factor[:, None]


def body(*arrays):
    return compute(*arrays)


def solution(mesh):
    fused = mesh.shape["samp"] == 4 and mesh.shape["bond"] == 4
    return jax.shard_map(
        sample_sites if fused else body,
        mesh=mesh,
        in_specs=(
            P(("parts", "samp"), "bond"),
            P("parts", "samp", None, None, "bond"),
            P("parts", None),
            P(("parts", "samp"), None),
        ),
        out_specs=(P(("parts", "samp"), None, None), P(("parts", "samp"), "bond")),
        check_vma=False,
    )
```

profile of v0, /device:TPU:0, one launch (start us, length us, event | category | flops | bytes accessed | tf_op | source)
XLA Modules:
  0.0 301.0 jit_solution(10397203690092737443)
XLA Ops:
  0.6 0.8 copy.8
  1.4 0.1 fusion.4
  1.5 0.6 gather_fusion
  2.0 0.1 copy.9
  2.1 0.1 fusion.2
  2.2 0.6 reshape.208.mask_ref
  2.8 1.7 copy.10.chosen_ref
  4.5 0.0 copy-start
  4.5 291.9 %shard_map.59 = (f32[512,1024]{1,0:T(8,128)}, f32[8,512]{1,0:T(8,128)}) custom-call(f32[32]{0:T(128)} %reshape.208.mask_ref, bf16[512,1024]{1,0:T(8,128)(2,1)} %env_ref.1, bf16[2,1,1024,4,1024]{4,3,2,1,0:T(4,128)(2,1)} %stored_ref.1, s32[2,512,1]{2,1,0:T(8,128)} %copy.10.chosen_ref), custom_call_target="tpu_custom_call" | custom-call | tf_op jit(solution)/shard_map/pallas_call | solution.py:621
  296.4 0.7 reshape.207
  297.2 0.0 copy-done
  297.3 0.6 pad_maximum_fusion
  297.9 3.1 %broadcast_multiply_fusion = f32[512,1024]{1,0:T(8,128)} fusion(f32[512,1024]{1,0:T(8,128)} %get-tuple-element.5, f32[512]{0:T(512)S(1)} %rsqrt_multiply_fusion), kind=kLoop, calls=%fused_computation.1 | loop fusion | flops 524288 | bytes 4196352 | tf_op jit(solution)/shard_map/mul | solution.py:674
  (8 shorter events, 0.1 us)
Async XLA Ops:
  4.5 292.7 %copy-start = (s32[512,2]{0,1:T(2,128)S(1)}, s32[512,2]{0,1:T(2,128)}, u32[]{:S(2)}) copy-start(s32[512,2]{0,1:T(2,128)} %param.7) | copy-start | bytes 12292
where the time goes:
time: 301 us
  Pallas kernels  292 us (97%)
  local copies, waits for them, and re-layouts  4.46 us (1%)
  other arithmetic  3.98 us (1%)
    pallas_call x1, Pallas kernels, sample_sites(): pl.pallas_call(functools.partial(sampling_kernel, bonds, groups), in_spec...  292 us

commit v1 on v0

--- a/solution.py
+++ b/solution.py
@@ -276,12 +276,12 @@
 MESH = pl.DeviceIdType.MESH
 PARTS_OF_SITE = 4
 SHARE = 4
-LEAD = 3
+EARLY = 10
 
 
 def sampling_kernel(
-    bonds, groups, mask_ref, env_ref, stored_ref, chosen_ref, selected_ref, totals_ref,
-    weights, blocks, foreign, picked, partial, answer, own, left, stage, norms, gathered,
+    bonds, groups, order_ref, env_ref, stored_ref, chosen_ref, selected_ref, totals_ref,
+    weights, blocks, foreign, picked, partial, answer, own, left, stage, norms, gathered, labels,
     env_sem, stage_sem, weight_send, weight_recv, gather_send, gather_recv, cross_send, cross_recv,
     spread_send, spread_recv, answer_send, answer_recv, norm_send, norm_recv,
 ):
@@ -324,13 +324,20 @@
         ref = blocks.at[site, peers[3], spot(chunk)]
         return copy_to(ref, ref, gather_send.at[unit, 1], gather_recv.at[unit, 1], {"bond": peers[1]})
 
-    def cross_whole(unit):
+    half = rows // 2
+
+    def first_hop(part, d):
+        ref, to = blocks.at[0, place, pl.ds(part * half, half)], part * units
+        return copy_to(ref, ref, gather_send.at[to, d - 1], gather_recv.at[to, d - 1], {"bond": peers[d]})
+
+    def first_relay(part):
+        ref, to = blocks.at[0, peers[3], pl.ds(part * half, half)], part * units
+        return copy_to(ref, ref, gather_send.at[to, 1], gather_recv.at[to, 1], {"bond": peers[1]})
+
+    def first_cross(part):
+        to, at = part * units, pl.ds(part * half, half)
         return copy_to(
-            picked.at[lax.rem(unit, 2)],
-            foreign.at[lax.rem(unit, chunks)],
-            cross_send.at[unit],
-            cross_recv.at[unit],
-            {"samp": opposite},
+            picked.at[0, :, at], foreign.at[0, :, at], cross_send.at[to], cross_recv.at[to], {"samp": opposite}
         )
 
     def band_of(position):
@@ -380,10 +387,12 @@
             weights.at[site, 0], weights.at[site, 1], weight_send.at[site], weight_recv.at[site], {"samp": sibling}
         )
 
+    owners = (mine, sibling, opposite, opposite + 1 - 2 * lax.rem(opposite, 2))
+
     def pick(site, which, at):
         total = None
         for block in range(bonds):
-            term = blocks[site, block, at, :].astype(jnp.float32) * mask_ref[(site * 4 + which) * bonds + block]
+            term = blocks[site, block, at, :].astype(jnp.float32) * jnp.where(order_ref[site, owners[which]] == block, 1.0, 0.0)
             total = term if total is None else total + term
         return total.astype(left.dtype)
 
@@ -400,6 +409,37 @@
         def _():
             hop(unit, 3).wait_recv()
             relay(unit).start()
+
+    def send_first(part):
+        first_hop(part, 1).start()
+        first_hop(part, 3).start()
+
+        @pl.when(outer)
+        def _():
+            first_hop(part, 2).start()
+
+    def forward_first(part):
+        @pl.when(middle)
+        def _():
+            first_hop(part, 3).wait_recv()
+            first_relay(part).start()
+
+    def cross_first(half_at):
+        first_hop(half_at, 1).wait_recv()
+        first_hop(half_at, 2).wait_recv()
+
+        @pl.when(outer)
+        def _():
+            first_hop(half_at, 3).wait_recv()
+
+        for part in range(2):
+
+            @pl.loop(0, half // band)
+            def _(step):
+                at = pl.ds(pl.multiple_of(half_at * half + step * band, band), band)
+                picked[0, part, at, :] = pick(0, 2 + part, at)
+
+        first_cross(half_at).start()
 
     def send_foreign(unit):
         site, chunk = split(unit)
@@ -414,36 +454,33 @@
 
         @pl.when(unit == 2)
         def _():
-            cross_whole(unit - 2).wait_send()
+            for part in range(2):
+                first_cross(part).wait_send()
 
         @pl.when(unit > 2)
         def _():
             cross_part(unit - 2).wait_send()
 
-        @pl.when(unit == 0)
-        def _():
-            for part in range(2):
-
-                @pl.loop(0, rows // band)
-                def _(step):
-                    at = pl.multiple_of(step * band, band)
-                    picked[slot, part, pl.ds(at, band), :] = pick(site, 2 + part, pl.ds(chunk * rows + at, band))
-
-            cross_whole(unit).start()
-
-        @pl.when(unit > 0)
-        def _():
-            at = pl.multiple_of(chunk * rows + lax.rem(place, SHARE) * share, share)
-            for part in range(2):
-                picked[slot, part, pl.ds(0, share), :] = pick(site, 2 + part, pl.ds(at, share))
-            cross_part(unit).start()
+        at = pl.multiple_of(chunk * rows + lax.rem(place, SHARE) * share, share)
+        for part in range(2):
+            picked[slot, part, pl.ds(0, share), :] = pick(site, 2 + part, pl.ds(at, share))
+        cross_part(unit).start()
 
     def spread_foreign(unit):
-        @pl.when(unit > 0)
-        def _():
-            cross_part(unit).wait_recv()
-            for d in range(1, SHARE):
-                spread(unit, d).start()
+        cross_part(unit).wait_recv()
+        spread(unit, 1).start()
+        spread(unit, 3).start()
+
+        @pl.when(outer)
+        def _():
+            spread(unit, 2).start()
+
+    def forward_foreign(unit):
+        @pl.when(middle)
+        def _():
+            spread(unit, 3).wait_recv()
+            ref = foreign.at[lax.rem(unit, chunks), :, band_of(peers[3])]
+            copy_to(ref, ref, spread_send.at[unit, 1], spread_recv.at[unit, 1], {"bond": peers[1]}).start()
 
     def multiply(unit):
         site, chunk = split(unit)
@@ -458,12 +495,18 @@
 
         @pl.when(unit == 0)
         def _():
-            cross_whole(unit).wait_recv()
+            for part in range(2):
+                first_cross(part).wait_recv()
 
         @pl.when(unit > 0)
         def _():
-            for d in range(1, SHARE):
-                spread(unit, d).wait_recv()
+            spread(unit, 1).wait_recv()
+            spread(unit, 2).wait_recv()
+
+            @pl.when(outer)
+            def _():
+                spread(unit, 3).wait_recv()
+
             for d in range(1, SHARE):
                 spread(unit, d).wait_send()
 
@@ -476,7 +519,11 @@
 
         @pl.loop(0, outcomes)
         def _(outcome):
-            @pl.when((outcome == outcomes // 2) & (unit + 1 < units))
+            @pl.when((outcome == outcomes // 2) & (unit == 0))
+            def _():
+                send_foreign(unit + 1)
+
+            @pl.when((outcome == outcomes // 2) & (unit > 0) & (unit + 1 < units))
             def _():
                 spread_foreign(unit + 1)
 
@@ -510,7 +557,7 @@
                 norm = jnp.sum(total * total, axis=1, keepdims=True)
                 lane = lax.broadcasted_iota(jnp.int32, (band, norms.shape[1]), 1)
                 norms[to, :] = jnp.where(lane == site * outcomes + outcome, norm, norms[to, :])
-                selected_ref[to, :] = jnp.where(chosen_ref[site, to, :] == outcome, total, selected_ref[to, :])
+                selected_ref[to, :] = jnp.where(labels[site, to, :1] == outcome, total, selected_ref[to, :])
 
         @pl.when(site + 1 < STEPS)
         def _():
@@ -540,43 +587,68 @@
     for friend in friends:
         pl.semaphore_signal(barrier, inc=1, device_id=friend, device_id_type=MESH)
     norms[...] = jnp.zeros_like(norms)
-    selected_ref[...] = jnp.zeros_like(selected_ref)
     first.wait()
     pl.semaphore_wait(barrier, len(friends))
 
-    each = -(-STEPS * tiles // (2 * LEAD))
-
-    @pl.loop(0, units + LEAD + 1)
-    def _(step):
-        now = step - LEAD
-
-        @pl.when((now + 2 >= 0) & (now + 2 < units))
-        def _():
-            forward_block(now + 2)
-
-        @pl.when((now + 1 >= 0) & (now + 1 < units))
-        def _():
-            send_foreign(now + 1)
-
-        @pl.when((now >= 0) & (now < units))
-        def _():
-            multiply(now)
-
-        @pl.when(now >= 1)
-        def _():
-            finish(now - 1)
-
-        @pl.when(now + 3 < units)
-        def _():
-            send_blocks(now + 3)
-
-        @pl.loop(0, each)
-        def _(turn):
-            index = step * each + turn
-
+    def shuffle_some(start, stop):
+        @pl.loop(start, stop)
+        def _(index):
             @pl.when(index < STEPS * tiles)
             def _():
                 shuffle(index)
+
+    send_first(0)
+    shuffle_some(0, 1)
+    forward_first(0)
+    send_first(1)
+    shuffle_some(1, 3)
+    forward_first(1)
+    send_blocks(1)
+    shuffle_some(3, 5)
+    cross_first(0)
+    shuffle_some(5, 7)
+    cross_first(1)
+    shuffle_some(7, EARLY)
+    selected_ref[...] = jnp.zeros_like(selected_ref)
+    for site in range(STEPS):
+        for chunk in range(chunks):
+            at = pl.ds(chunk * rows, rows)
+            wide = jnp.broadcast_to(chosen_ref[site : site + 1, at], (128, rows))
+            labels[site, at, :] = jnp.transpose(wide)
+    forward_block(1)
+    send_blocks(2)
+
+    @pl.loop(0, units + 1)
+    def _(now):
+        @pl.when((now > 0) & (now + 1 < units))
+        def _():
+            send_foreign(now + 1)
+
+        @pl.when(now < units)
+        def _():
+            multiply(now)
+
+        @pl.when(now >= 1)
+        def _():
+            finish(now - 1)
+
+        @pl.when(now == 0)
+        def _():
+            spread_foreign(now + 1)
+
+        @pl.when(now + 2 < units)
+        def _():
+            forward_block(now + 2)
+
+        @pl.when(now + 1 < units)
+        def _():
+            forward_foreign(now + 1)
+
+        @pl.when(now + 3 < units)
+        def _():
+            send_blocks(now + 3)
+
+        shuffle_some(EARLY + 2 * now, EARLY + 2 * now + 2)
 
     for chunk in range(chunks):
         at = pl.ds(chunk * rows, rows)
@@ -590,10 +662,14 @@
     for site in range(STEPS):
         trade_all(site).wait_send()
 
-    @pl.loop(0, units)
+    @pl.loop(1, units)
     def _(unit):
         for d in range(1, bonds):
             hop(unit, d).wait_send()
+
+    for part in range(2):
+        for d in range(1, bonds):
+            first_hop(part, d).wait_send()
 
     for unit in range(units - 2, units):
         cross_part(unit).wait_send()
@@ -606,16 +682,11 @@
 
 def sample_sites(env_start, stored_sites, slab_order, chosen):
     groups, bonds = slab_order.shape[1], lax.axis_size("bond")
-    mine = lax.axis_index("samp")
     slab, outcomes, width = stored_sites.shape[2:]
     samples = env_start.shape[0]
     rows = samples // PARTS_OF_SITE
     units = STEPS * PARTS_OF_SITE
     tall = min(slab, 128)
-    sibling, opposite = mine + 1 - 2 * (mine % 2), (mine + groups // 2) % groups
-    opposite_sibling = opposite + 1 - 2 * (opposite % 2)
-    wanted = slab_order[:, jnp.stack([mine, sibling, opposite, opposite_sibling])]
-    mask = (wanted[:, :, None] == jnp.arange(bonds, dtype=jnp.int32)).astype(jnp.float32).reshape(-1)
     kind = env_start.dtype
     dma = pltpu.SemaphoreType.DMA
     selected, totals = pl.pallas_call(
@@ -643,14 +714,15 @@
             pltpu.VMEM((2, tall, outcomes, width), kind),
             pltpu.VMEM((samples, 128), jnp.float32),
             pltpu.VMEM((bonds, STEPS * outcomes, samples), jnp.float32),
+            pltpu.VMEM((STEPS, samples, 128), jnp.int32),
             dma,
             dma((2,)),
             dma((STEPS,)),
             dma((STEPS,)),
-            dma((units, bonds - 1)),
-            dma((units, bonds - 1)),
-            dma((units,)),
-            dma((units,)),
+            dma((units + 1, bonds - 1)),
+            dma((units + 1, bonds - 1)),
+            dma((units + 1,)),
+            dma((units + 1,)),
             dma((units, bonds - 1)),
             dma((units, bonds - 1)),
             dma((units, outcomes)),
@@ -661,7 +733,7 @@
         compiler_params=pltpu.CompilerParams(
             collective_id=0, has_side_effects=True, vmem_limit_bytes=67_000_000
         ),
-    )(mask, env_start, stored_sites, jnp.transpose(chosen)[:, :, None])
+    )(slab_order, env_start, stored_sites, jnp.transpose(chosen))
     totals = jnp.transpose(totals).reshape(samples, STEPS, outcomes)
     factor = jnp.ones((samples,), jnp.float32)
     labels = jnp.arange(outcomes, dtype=jnp.int32)

time: 301 us -> 257 us (0.85)
  Pallas kernels: 292 us -> 251 us
  local copies, waits for them, and re-layouts: 4.46 us -> 0.74 us
    pallas_call x1, Pallas kernels: 292 us -> 251 us  [sample_sites(): pl.pallas_call(functools.partial(sampling_kernel, bonds, groups), in_spec...]
where the time goes in v1:
time: 257 us
  Pallas kernels  251 us (98%)
  other arithmetic  3.82 us (1%)
    pallas_call x1, Pallas kernels, sample_sites(): pl.pallas_call(functools.partial(sampling_kernel, bonds, groups), in_spec...  251 us

profile of v1, /device:TPU:0, one launch (start us, length us, event | category | flops | bytes accessed | tf_op | source)
XLA Modules:
  0.0 256.6 jit_solution(7606141214912807075)
XLA Ops:
  0.6 0.0 copy-start
  0.6 251.3 %shard_map.59 = (f32[512,1024]{1,0:T(8,128)}, f32[8,512]{1,0:T(8,128)}) custom-call(s32[2,4]{1,0:T(2,128)} %order_ref.1, bf16[512,1024]{1,0:T(8,128)(2,1)} %env_ref.1, bf16[2,1,1024,4,1024]{4,3,2,1,0:T(4,128)(2,1)} %stored_ref.1, s32[2,512]{1,0:T(2,128)} %bitcast.16), custom_call_target="tpu_custom_call" | custom-call | tf_op jit(solution)/shard_map/pallas_call | solution.py:692
  252.0 0.7 reshape.39
  252.7 0.0 copy-done
  252.8 0.6 pad_maximum_fusion
  253.4 3.1 %broadcast_multiply_fusion = f32[512,1024]{1,0:T(8,128)} fusion(f32[512,1024]{1,0:T(8,128)} %get-tuple-element.5, f32[512]{0:T(512)S(1)} %rsqrt_multiply_fusion), kind=kLoop, calls=%fused_computation | loop fusion | flops 524288 | bytes 4196352 | tf_op jit(solution)/shard_map/mul | solution.py:746
  (7 shorter events, 0.1 us)
Async XLA Ops:
  0.6 252.1 %copy-start = (s32[512,2]{0,1:T(2,128)S(1)}, s32[512,2]{0,1:T(2,128)}, u32[]{:S(2)}) copy-start(s32[512,2]{0,1:T(2,128)} %param.7) | copy-start | bytes 12292
